TPU v7x, 32 devices: a whole 2x2x4 slice. The times are simulated.
32 devices in a mesh: dp: 4 (over z), seq: 8 (over y, x, core).
Axes of the slice: x: 2, y: 2, z: 4, core: 2. Of those that a mesh axis runs over, the one named last changes fastest.
Arguments:
- tiles: bfloat16 [4, 1536, 768], P('dp', 'seq'), may hold values from -40 to 40
- cotangent: bfloat16 [4, 1536, 768], P('dp', 'seq'), may hold values from -0.078125 to 0.078125
- segment_of: int32 [4, 1536, 1], P('dp', 'seq'), may hold values from 0 to 15; in each aligned block of 192 rows (0 to 191, 192 to 383, ..., all dimensions but the last counted through in order) at most 20 rows name the same one
- tissue_count: int32 [4], P('dp'), may hold values from 768 to 1536
- w_query: bfloat16 [768, 768], P('seq'), may hold values from -0.21875 to 0.21875
- w_key: bfloat16 [768, 768], P('seq'), may hold values from -0.21875 to 0.21875
- w_value: bfloat16 [768, 768], P('seq'), may hold values from -0.21875 to 0.21875
- w_out: bfloat16 [768, 768], P('seq'), may hold values from -2.390625 to 2.390625
Outputs:
- layer_out: bfloat16 [4, 1536, 768], P('dp', 'seq')
- grad_value: float32 [768, 768], P('seq')
Inputs may be any that keep to these rules, and one draw needn't show every extreme that they name: `segment_of`: within one slide, the 192 tiles of one block name one group at most 20 times; some group is named exactly 20 times.
All inputs are finite; a program needn't handle non-finite values.
Results may differ from a plain program's by a relative error of at most 0.014.
Values may be sent and summed in bfloat16 or wider, within the bound.
No kernel may reach another device: no remote copies, remote signals or barrier semaphores. Data moves between devices by JAX's collectives and lax.ppermute only.
A program may use at most 64 MiB of HBM per device.

v0:
```python
import jax
import jax.numpy as jnp
from jax import lax
from jax.sharding import PartitionSpec as P

HEADS = 12
SEG_DEV = 2
NEG_BIG = -1e30


def contract_last(left, right):
    return lax.dot_general(
        left, right, (((1,), (1,)), ((), ())), preferred_element_type=jnp.float32
    )


def contract_first(left, right):
    return lax.dot_general(
        left, right, (((0,), (0,)), ((), ())), preferred_element_type=jnp.float32
    )


def local(tiles, cotangent, segment_of, tissue_count, w_query, w_key, w_value, w_out):
    rows = tiles.shape[1]
    width = tiles.shape[2]
    heads = HEADS
    head_dim = width // heads
    scale = head_dim ** (-0.5)
    seq_count = lax.axis_size("seq")
    own_index = lax.axis_index("seq")
    segments = SEG_DEV * seq_count
    capacity = 5 * rows // (3 * segments)
    slots = segments * capacity
    per_segment = seq_count * capacity
    full_query, full_key, full_value, full_out = (
        lax.all_gather(w_query, "seq", axis=0, tiled=True),
        lax.all_gather(w_key, "seq", axis=0, tiled=True),
        lax.all_gather(w_value, "seq", axis=0, tiled=True),
        lax.all_gather(w_out, "seq", axis=0, tiled=True),
    )
    inputs = tiles[0]
    position = own_index * rows + jnp.arange(rows, dtype=jnp.int32)
    inside = position < tissue_count[0]
    masked_cot = cotangent[0] * inside[:, None].astype(jnp.bfloat16)
    query_rows = jnp.dot(inputs, full_query, preferred_element_type=jnp.float32).astype(
        jnp.bfloat16
    )
    key_rows = jnp.dot(inputs, full_key, preferred_element_type=jnp.float32).astype(jnp.bfloat16)
    value_rows = jnp.dot(inputs, full_value, preferred_element_type=jnp.float32).astype(
        jnp.bfloat16
    )
    dout_rows = contract_last(masked_cot, full_out).astype(jnp.bfloat16)

    def by_heads(block):
        return block.reshape(rows, heads, head_dim).transpose(1, 0, 2)

    query_heads = by_heads(query_rows)
    key_heads = by_heads(key_rows)
    visible = inside[None, :] | jnp.eye(rows, dtype=bool)

    def local_scores(query_one, key_one):
        scores = contract_last(query_one, key_one) * scale
        return jnp.where(visible, scores, NEG_BIG)

    def local_stats(pair):
        scores = local_scores(pair[0], pair[1])
        top = jnp.max(scores, axis=1)
        total = jnp.sum(jnp.exp(scores - top[:, None]), axis=1)
        return (top, total)

    local_max, local_sum = lax.map(local_stats, (query_heads, key_heads))
    stats_rows = jnp.stack([local_max.T, local_sum.T], axis=1)
    segment_rows = segment_of[0, :, 0]
    member = (segment_rows[:, None] == jnp.arange(segments, dtype=jnp.int32)[None, :]).astype(
        jnp.int32
    )
    rank = jnp.sum(jnp.cumsum(member, axis=0) * member, axis=1) - 1
    slot_index = segment_rows * capacity + rank
    source_row = (
        jnp.full((slots,), rows, jnp.int32).at[slot_index].set(jnp.arange(rows, dtype=jnp.int32))
    )
    state_rows = jnp.where(inside, 2, 1).astype(jnp.int32)

    def to_slots(block):
        padded = jnp.concatenate([block, jnp.zeros((1,) + block.shape[1:], block.dtype)], axis=0)
        gathered = jnp.take(padded, source_row, axis=0)
        return gathered.reshape((seq_count, SEG_DEV, capacity) + block.shape[1:])

    members = [query_rows, key_rows, value_rows, dout_rows]
    bulk_rows = jnp.stack(members, axis=1)

    def unpack(bulk_one):
        return (bulk_one[:, 0], bulk_one[:, 1], bulk_one[:, 2], bulk_one[:, 3])

    send_bulk = to_slots(bulk_rows)
    send_stats = to_slots(stats_rows)
    send_state = to_slots(state_rows)
    eye_slots = jnp.eye(per_segment, dtype=bool)
    bulk = lax.all_to_all(
        send_bulk.astype(jnp.float32), "seq", split_axis=0, concat_axis=2, tiled=True
    ).astype(send_bulk.dtype)
    stats = lax.all_to_all(send_stats, "seq", split_axis=0, concat_axis=2, tiled=True)
    state = lax.all_to_all(send_state, "seq", split_axis=0, concat_axis=2, tiled=True)

    def one_segment(item):
        bulk_one, stats_one, state_one = item
        query_seg, key_seg, value_seg, dout_seg = unpack(bulk_one)
        slot_count = query_seg.shape[0]
        query_seg = query_seg.reshape(slot_count, heads, head_dim)
        key_seg = key_seg.reshape(slot_count, heads, head_dim)
        value_seg = value_seg.reshape(slot_count, heads, head_dim)
        dout_seg = dout_seg.reshape(slot_count, heads, head_dim)
        seen = (state_one == 2)[None, :] | eye_slots
        scores = (
            jnp.einsum("qhc,khc->hqk", query_seg, key_seg, preferred_element_type=jnp.float32)
            * scale
        )
        scores = jnp.where(seen[None], scores, NEG_BIG)
        far_max = jnp.max(scores, axis=2)
        far_sum = jnp.sum(jnp.exp(scores - far_max[:, :, None]), axis=2)
        seg_near_max = stats_one[:, 0, :].T
        seg_near_sum = stats_one[:, 1, :].T
        top = jnp.maximum(far_max, seg_near_max)
        log_total = top + jnp.log(
            seg_near_sum * jnp.exp(seg_near_max - top) + far_sum * jnp.exp(far_max - top)
        )
        weights = jnp.exp(scores - log_total[:, :, None]).astype(jnp.bfloat16)
        far_out = jnp.einsum("hqk,khc->qhc", weights, value_seg, preferred_element_type=jnp.float32)
        far_grad = jnp.einsum("hqk,qhc->khc", weights, dout_seg, preferred_element_type=jnp.float32)
        far_out = far_out.astype(jnp.bfloat16).reshape(slot_count, width)
        far_grad = far_grad.astype(jnp.bfloat16).reshape(slot_count, width)
        return (far_out, far_grad, log_total.T)

    far_out, far_grad, totals = lax.map(one_segment, (bulk[0], stats[0], state[0]))
    back_bulk = jnp.stack([far_out, far_grad], axis=2)[None]
    back_lse = totals[None]
    home_bulk, home_lse = (
        lax.all_to_all(
            back_bulk.astype(jnp.float32), "seq", split_axis=2, concat_axis=0, tiled=True
        ).astype(back_bulk.dtype),
        lax.all_to_all(back_lse, "seq", split_axis=2, concat_axis=0, tiled=True),
    )
    far_rows = jnp.take(home_bulk.reshape((slots,) + back_bulk.shape[3:]), slot_index, axis=0)
    lse_rows = jnp.take(home_lse.reshape(slots, heads), slot_index, axis=0)

    def local_apply(item):
        query_one, key_one, value_one, dout_one, lse_one = item
        scores = local_scores(query_one, key_one)
        weights = jnp.exp(scores - lse_one[:, None]).astype(jnp.bfloat16)
        near_out = jnp.dot(weights, value_one, preferred_element_type=jnp.float32)
        near_grad = contract_first(weights, dout_one)
        return (near_out, near_grad)

    near_out, near_grad = lax.map(
        local_apply, (query_heads, key_heads, by_heads(value_rows), by_heads(dout_rows), lse_rows.T)
    )
    near_grad = near_grad.transpose(1, 0, 2).reshape(rows, width).astype(jnp.bfloat16)
    far_out_rows = far_rows[:, 0]
    grad_right = far_rows[:, 1]
    attention = (
        near_out.transpose(1, 0, 2).reshape(rows, width) + far_out_rows.astype(jnp.float32)
    ).astype(jnp.bfloat16)
    layer_rows = jnp.dot(attention, full_out, preferred_element_type=jnp.float32).astype(
        jnp.bfloat16
    )
    grad_part = lax.psum_scatter(
        (contract_first(inputs, near_grad) + contract_first(inputs, grad_right)).astype(
            jnp.bfloat16
        ),
        "seq",
        scatter_dimension=0,
        tiled=True,
    ).astype(jnp.float32)
    grad_part = lax.psum(grad_part.astype(jnp.bfloat16), "dp").astype(jnp.float32)
    return (layer_rows[None], grad_part)


def solution(mesh):
    placed = (
        P("dp", "seq", None),
        P("dp", "seq", None),
        P("dp", "seq", None),
        P("dp"),
        P("seq", None),
        P("seq", None),
        P("seq", None),
        P("seq", None),
    )
    return jax.shard_map(
        local,
        mesh=mesh,
        in_specs=placed,
        out_specs=(P("dp", "seq", None), P("seq", None)),
        check_vma=False,
    )
```

profile of v0, /device:TPU:0, one launch (start us, length us, event | category | flops | bytes accessed | tf_op | source)
XLA Modules:
  0.0 328.2 jit_solution(14311517233252371151)
XLA Ops:
  14.5 2.5 gather_fusion.1
  17.6 5.2 %all-to-all-start.1 = ((s32[8,2,20]{2,1,0:T(2,128)}), s32[8,2,20]{2,1,0:T(2,128)S(1)}, u32[]{:S(2)}, u32[]{:S(2)}) async-start(s32[8,2,20]{2,1,0:T(2,128)} %broadcast_select_fusion.2), calls=%async_computation.1 | async-start | bytes 16384 | tf_op jit(solution)/shard_map/all_to_all | solution.py:103
  23.4 13.1 %all-gather.5.cloned.1.call-done = bf16[768,768]{1,0:T(8,128)(2,1)} async-done(((bf16[96,768]{1,0:T(8,128)(2,1)}), bf16[768,768]{1,0:T(8,128)(2,1)}) %all-gather.5.cloned.1.call-update) | async-done | bytes 1179664 | tf_op jit(solution)/shard_map/all_gather | solution.py:36
  38.7 23.7 %all-gather.7.cloned.1.call-done = bf16[768,768]{1,0:T(8,128)(2,1)} async-done(((bf16[96,768]{1,0:T(8,128)(2,1)}), bf16[768,768]{1,0:T(8,128)(2,1)}) %all-gather.7.cloned.1.call-update) | async-done | bytes 1179664 | tf_op jit(solution)/shard_map/all_gather | solution.py:37
  64.5 4.9 %while.41 = (s32[]{:T(128)}, f32[12,192]{1,0:T(8,128)S(1)}, f32[12,192]{1,0:T(8,128)S(1)}, bf16[12,192,64]{2,1,0:T(8,128)(2,1)S(1)}, bf16[12,192,64]{2,1,0:T(8,1...) while((s32[]{:T(128)}, f32[12,192]{1,0:T(8,128)S(1)}, ...), condition=%wide.region_7.8_spmd.clone, body=%wide.region_4.7_spmd.clone.sunk | while | flops 4976258 | bytes 400221 | solution.py:71
  70.5 2.0 gather_fusion.2
  73.0 15.2 %all-gather.9.cloned.1.call-done = bf16[768,768]{1,0:T(8,128)(2,1)} async-done(((bf16[96,768]{1,0:T(8,128)(2,1)}), bf16[768,768]{1,0:T(8,128)(2,1)}) %all-gather.9.cloned.1.call-update) | async-done | bytes 1179664 | tf_op jit(solution)/shard_map/all_gather | solution.py:38
  89.9 24.0 %all-gather.11.cloned.1.call-done = bf16[768,768]{1,0:T(8,128)(2,1)} async-done(((bf16[96,768]{1,0:T(8,128)(2,1)}), bf16[768,768]{1,0:T(8,128)(2,1)}) %all-gather.11.cloned.1.call-update) | async-done | bytes 1179664 | tf_op jit(solution)/shard_map/all_gather | solution.py:39
  118.9 3.9 %gather_fusion = bf16[320,4,768]{2,1,0:T(4,128)(2,1)S(1)} fusion(bf16[193,4,768]{2,1,0:T(4,128)(2,1)S(1)} %concatenate.16.clone, s32[1024]{0:T(1024)S(1)} %pad_clamp_fusion.1), kind=kCustom, calls=%fused_computation | custom fusion | bytes 3933440 | tf_op jit(solution)/shard_map/jit(_take)/gather | solution.py:86
  122.9 3.3 %all-to-all-start.2 = ((f32[8,1,960]{2,1,0:T(1,128)}), f32[8,1,960]{2,1,0:T(1,128)S(1)}, u32[]{:S(2)}, u32[]{:S(2)}) async-start(f32[8,1,960]{2,1,0:T(1,128)} %reshape.247), calls=%async_computation.2 | async-start | bytes 65536 | tf_op jit(solution)/shard_map/all_to_all | solution.py:102
  126.2 2.1 select_convert_fusion
  128.3 2.6 all-to-all-done.2
  131.0 3.8 %all-to-all-start = ((bf16[8,2,20,4,768]{4,3,2,1,0:T(4,128)(2,1)}), bf16[8,2,20,4,768]{4,3,2,1,0:T(4,128)(2,1)S(1)}, u32[]{:S(2)}, u32[]{:S(2)}) async-start(bf16[8,2,20,4,768]{4,3,2,1,0:T(4,128)(2,1)} %select_convert_fusion), calls=%async_computation | async-start | bytes 3932160 | tf_op jit(solution)/shard_map/all_to_all | solution.py:99
  138.6 21.1 %all-to-all-done = bf16[8,2,20,4,768]{4,3,2,1,0:T(4,128)(2,1)S(1)} async-done(((bf16[8,2,20,4,768]{4,3,2,1,0:T(4,128)(2,1)}), bf16[8,2,20,4,768]{4,3,2,1,0:T(4,128)(2,1)S(1)}, u32[]{:S(2)}, u32[]{:S(2)}) %all-to-all-start) | async-done | bytes 1966112 | tf_op jit(solution)/shard_map/all_to_all | solution.py:99
  159.7 2.0 copy.124
  161.7 11.5 %while.42 = (s32[]{:T(128)}, bf16[2,160,768]{2,1,0:T(8,128)(2,1)}, bf16[2,160,768]{2,1,0:T(8,128)(2,1)}, f32[2,160,12]{1,2,0:T(8,128)S(1)}, bf16[2,160,4,768]{3,...) while((s32[]{:T(128)}, bf16[2,160,768]{2,1,0:T(8,128)(2,1)}, ...), condition=%wide.region_11.12_spmd.clone, body=%wide.region_8.11_spmd.clone.sunk | while | flops 121049760 | bytes 14496293 | solution.py:134
  174.2 3.3 %all-to-all-start.3 = ((f32[8,1,480]{2,1,0:T(1,128)}), f32[8,1,480]{2,1,0:T(1,128)S(1)}, u32[]{:S(2)}, u32[]{:S(2)}) async-start(f32[8,1,480]{2,1,0:T(1,128)} %reshape.249), calls=%async_computation.3 | async-start | bytes 32768 | tf_op jit(solution)/shard_map/all_to_all | solution.py:141
  178.9 2.0 copy.147
  182.3 4.2 %all-to-all-start.4 = ((bf16[1,2,160,2,768]{4,3,1,0,2:T(2,128)(2,1)}), bf16[1,2,160,2,768]{4,3,1,0,2:T(2,128)(2,1)}, u32[]{:S(2)}, u32[]{:S(2)}) async-start(bf16[1,2,160,2,768]{4,3,1,0,2:T(2,128)(2,1)} %copy.147), calls=%async_computation.4 | async-start | bytes 1966080 | tf_op jit(solution)/shard_map/all_to_all | solution.py:138
  189.1 42.2 %while.43 = (s32[]{:T(128)}, f32[12,192,64]{1,2,0:T(8,128)}, bf16[12,192,64]{1,2,0:T(8,128)(2,1)S(1)}, bf16[12,192,64]{2,1,0:T(8,128)(2,1)}, bf16[12,192,64]{2,1...) while((s32[]{:T(128)}, f32[12,192,64]{1,2,0:T(8,128)}, ...), condition=%wide.region_13.14_spmd.clone, body=%wide.region_12.13_spmd.clone.sunk | while | flops 14376962 | bytes 546345 | solution.py:154
  235.4 3.1 gather_fusion.4
  241.5 2.4 copy.157
  245.4 36.4 %reduce-scatter.4.cloned.1.call-done = bf16[96,768]{1,0:T(8,128)(2,1)} async-done(((bf16[768,768]{1,0:T(8,128)(2,1)}), bf16[96,768]{1,0:T(8,128)(2,1)}) %reduce-scatter.4.cloned.1.call-update) | async-done | bytes 147472
  284.7 34.9 %all-reduce.5.cloned.1.call-done = bf16[96,768]{0,1:T(8,128)(2,1)} async-done(((bf16[96,768]{0,1:T(8,128)(2,1)}), bf16[96,768]{0,1:T(8,128)(2,1)}) %all-reduce.5.cloned.1.call-update) | async-done | bytes 147472 | tf_op jit(solution)/shard_map/psum | solution.py:174
  (245 shorter events, 101.3 us)
Async XLA Ops:
  7.2 29.4 %copy-start = (bf16[1,192,768]{2,1,0:T(8,128)(2,1)S(1)}, bf16[1,192,768]{2,1,0:T(8,128)(2,1)}, u32[]{:S(2)}) copy-start(bf16[1,192,768]{2,1,0:T(8,128)(2,1)} %param.14) | copy-start | bytes 884740
  7.2 29.4 %all-gather.5.cloned.1.call-start = ((), (), s32[]{:S(2)}) async-start(), calls=%async_computation.6 | async-start | bytes 1327104 | tf_op jit(solution)/shard_map/all_gather | solution.py:36
  7.9 54.5 %all-gather.7.cloned.1.call-start = ((), (), s32[]{:S(2)}) async-start(), calls=%async_computation.7 | async-start | bytes 1327104 | tf_op jit(solution)/shard_map/all_gather | solution.py:37
  8.7 79.6 %all-gather.9.cloned.1.call-start = ((), (), s32[]{:S(2)}) async-start(), calls=%async_computation.8 | async-start | bytes 1327104 | tf_op jit(solution)/shard_map/all_gather | solution.py:38
  17.6 105.2 %all-to-all-start.1 = ((s32[8,2,20]{2,1,0:T(2,128)}), s32[8,2,20]{2,1,0:T(2,128)S(1)}, u32[]{:S(2)}, u32[]{:S(2)}) async-start(s32[8,2,20]{2,1,0:T(2,128)} %broadcast_select_fusion.2), calls=%async_computation.1 | async-start | bytes 16384 | tf_op jit(solution)/shard_map/all_to_all | solution.py:103
  22.8 91.1 %all-gather.11.cloned.1.call-start = ((), (), s32[]{:S(2)}) async-start(), calls=%async_computation.9 | async-start | bytes 1327104 | tf_op jit(solution)/shard_map/all_gather | solution.py:39
  69.4 0.8 copy-start.6
  69.4 3.1 copy-start.7
  70.3 43.6 %copy-start.9 = (bf16[1,192,768]{2,1,0:T(8,128)(2,1)S(1)}, bf16[1,192,768]{2,1,0:T(8,128)(2,1)}, u32[]{:S(2)}) copy-start(bf16[1,192,768]{2,1,0:T(8,128)(2,1)} %param.15) | copy-start | bytes 884740
  89.9 26.7 %copy-start.2 = (bf16[192,768]{1,0:T(8,128)(2,1)}, bf16[192,768]{1,0:T(8,128)(2,1)S(1)}, u32[]{:S(2)}) copy-start(bf16[192,768]{1,0:T(8,128)(2,1)S(1)} %convolution_convert_fusion.4) | copy-start | bytes 884740
  115.7 0.7 copy-start.4
  122.9 8.1 %all-to-all-start.2 = ((f32[8,1,960]{2,1,0:T(1,128)}), f32[8,1,960]{2,1,0:T(1,128)S(1)}, u32[]{:S(2)}, u32[]{:S(2)}) async-start(f32[8,1,960]{2,1,0:T(1,128)} %reshape.247), calls=%async_computation.2 | async-start | bytes 65536 | tf_op jit(solution)/shard_map/all_to_all | solution.py:102
  128.3 6.5 %copy-start.10 = (s32[1,192,1]{1,2,0:T(1,128)S(1)}, s32[1,192,1]{1,2,0:T(1,128)}, u32[]{:S(2)}) copy-start(s32[1,192,1]{1,2,0:T(1,128)} %param.16) | copy-start | bytes 2308
  128.3 6.6 %copy-start.5 = (bf16[192,768]{1,0:T(8,128)(2,1)S(1)}, bf16[192,768]{1,0:T(8,128)(2,1)}, u32[]{:S(2)}) copy-start(bf16[192,768]{1,0:T(8,128)(2,1)} %copy-done.4) | copy-start | bytes 884740
  128.3 7.5 %copy-start.3 = (bf16[192,768]{1,0:T(8,128)(2,1)S(1)}, bf16[192,768]{1,0:T(8,128)(2,1)}, u32[]{:S(2)}) copy-start(bf16[192,768]{1,0:T(8,128)(2,1)} %copy-done.2) | copy-start | bytes 884740
  131.0 28.7 %all-to-all-start = ((bf16[8,2,20,4,768]{4,3,2,1,0:T(4,128)(2,1)}), bf16[8,2,20,4,768]{4,3,2,1,0:T(4,128)(2,1)S(1)}, u32[]{:S(2)}, u32[]{:S(2)}) async-start(bf16[8,2,20,4,768]{4,3,2,1,0:T(4,128)(2,1)} %select_convert_fusion), calls=%async_computation | async-start | bytes 3932160 | tf_op jit(solution)/shard_map/all_to_all | solution.py:99
  174.2 8.0 %all-to-all-start.3 = ((f32[8,1,480]{2,1,0:T(1,128)}), f32[8,1,480]{2,1,0:T(1,128)S(1)}, u32[]{:S(2)}, u32[]{:S(2)}) async-start(f32[8,1,480]{2,1,0:T(1,128)} %reshape.249), calls=%async_computation.3 | async-start | bytes 32768 | tf_op jit(solution)/shard_map/all_to_all | solution.py:141
  180.9 8.3 %copy-start.8 = (bf16[12,192,64]{1,2,0:T(8,128)(2,1)S(1)}, bf16[12,192,64]{1,2,0:T(8,128)(2,1)}, u32[]{:S(2)}) copy-start(bf16[12,192,64]{1,2,0:T(8,128)(2,1)} %custom-call.16) | copy-start | bytes 884740
  182.3 49.6 %all-to-all-start.4 = ((bf16[1,2,160,2,768]{4,3,1,0,2:T(2,128)(2,1)}), bf16[1,2,160,2,768]{4,3,1,0,2:T(2,128)(2,1)}, u32[]{:S(2)}, u32[]{:S(2)}) async-start(bf16[1,2,160,2,768]{4,3,1,0,2:T(2,128)(2,1)} %copy.147), calls=%async_computation.4 | async-start | bytes 1966080 | tf_op jit(solution)/shard_map/all_to_all | solution.py:138
  186.5 95.3 %reduce-scatter.4.cloned.1.call-start = ((), (), s32[]{:S(2)}) async-start(), calls=%async_computation.11 | async-start | bytes 1327104
  243.8 39.7 %copy-start.1 = (bf16[768,768]{1,0:T(8,128)(2,1)S(1)}, bf16[768,768]{1,0:T(8,128)(2,1)}, u32[]{:S(2)}) copy-start(bf16[768,768]{1,0:T(8,128)(2,1)} %all-gather.11.cloned.1.call-done) | copy-start | bytes 3538948
  243.9 75.7 %all-reduce.5.cloned.1.call-start = ((), (), s32[]{:S(2)}) async-start(), calls=%async_computation.10 | async-start | bytes 393216 | tf_op jit(solution)/shard_map/psum | solution.py:174
Sparse Core Ops, SparseCore 0:
  9.9 26.6 all-gather.4
  38.4 23.9 all-gather.6
  64.3 23.9 all-gather.8
  90.0 23.9 all-gather.10
  244.0 37.7 reduce-scatter.3
  284.5 34.9 all-reduce.4
where the time goes:
time: 331 us; the launch traced here: 328 us
  waiting for transfers between devices  175 us (53%)
  matrix products  57.6 us (17%)
  local copies, waits for them, and re-layouts  47.3 us (14%)
  starting transfers between devices  20.3 us (6%)
  between operations  15.3 us (5%)
  other arithmetic  11.8 us (4%)
    unnamed x7, waiting for transfers between devices  39 us
    psum x1, waiting for transfers between devices, local(): lax.psum(grad_part.astype(jnp.bfloat16), 'dp').astype(jnp.float32)  34.9 us
    all_gather x1, waiting for transfers between devices, local(): lax.all_gather(w_out, 'seq', axis=0, tiled=True)  24 us
    all_gather x1, waiting for transfers between devices, local(): lax.all_gather(w_key, 'seq', axis=0, tiled=True)  23.7 us
    all_to_all x1, waiting for transfers between devices, local(): lax.all_to_all(send_bulk.astype(jnp.float32), 'seq', split_axis=0, concat...  21.1 us
    dot_general x12, matrix products, local_apply(): near_out = jnp.dot(weights, value_one, preferred_element_type=jnp.float32)  18.6 us
    dot_general x25, matrix products, contract_last(): lax.dot_general(left, right, (((1,), (1,)), ((), ())), preferred_element_...  17.2 us
    all_gather x1, waiting for transfers between devices, local(): lax.all_gather(w_value, 'seq', axis=0, tiled=True)  15.2 us
  transfers between devices with their start and end apart: 11, of which 9 were waited for; matrix products, arithmetic and copies ran while one was open for 26% of the time, Pallas kernels for 0%

commit v1 on v0

--- a/solution.py
+++ b/solution.py
@@ -1,3 +1,4 @@
+import functools
 import jax
 import jax.numpy as jnp
 from jax import lax
@@ -6,6 +7,16 @@
 HEADS = 12
 SEG_DEV = 2
 NEG_BIG = -1e30
+
+
+def _mix_targets(local_x, which_axis):
+    back = jax.lax.axis_size(which_axis)
+    b_next = jnp.split(local_x, back, 0)
+    local_out = jnp.stack(b_next, 0)
+    return jnp.concatenate(jax.lax.all_to_all(local_out, which_axis, 0, 0), 2)
+
+
+switch_targets = functools.partial(_mix_targets, which_axis="seq")
 
 
 def contract_last(left, right):
@@ -96,9 +107,7 @@
     send_stats = to_slots(stats_rows)
     send_state = to_slots(state_rows)
     eye_slots = jnp.eye(per_segment, dtype=bool)
-    bulk = lax.all_to_all(
-        send_bulk.astype(jnp.float32), "seq", split_axis=0, concat_axis=2, tiled=True
-    ).astype(send_bulk.dtype)
+    bulk = switch_targets(send_bulk.astype(jnp.float32)).astype(send_bulk.dtype)
     stats = lax.all_to_all(send_stats, "seq", split_axis=0, concat_axis=2, tiled=True)
     state = lax.all_to_all(send_state, "seq", split_axis=0, concat_axis=2, tiled=True)
 

time: 331 us -> 362 us (1.094)
  waiting for transfers between devices: 175 us -> 185 us
  matrix products: 57.6 us -> 67.1 us
  local copies, waits for them, and re-layouts: 47.3 us -> 56.5 us
    dot_general x25, matrix products: 17.2 us -> 26.8 us  [contract_last(): lax.dot_general(left, right, (((1,), (1,)), ((), ())), preferred_element_...]
    all_gather x1, waiting for transfers between devices: 15.2 us -> 23.2 us  [local(): lax.all_gather(w_value, 'seq', axis=0, tiled=True)]
    unnamed x36 -> x33, local copies, waits for them, and re-layouts: 11.5 us -> 18 us
  transfers between devices with their start and end apart: 11 -> 11, of which waited for: 9 -> 9; matrix products, arithmetic and copies ran while one was open for 26% -> 30% of each run, Pallas kernels for 0% -> 0%
where the time goes in v1:
time: 362 us; the launch traced here: 358 us
  waiting for transfers between devices  185 us (51%)
  matrix products  67.1 us (19%)
  local copies, waits for them, and re-layouts  56.5 us (16%)
  starting transfers between devices  20.3 us (6%)
  between operations  15.2 us (4%)
  other arithmetic  13 us (4%)
    unnamed x7, waiting for transfers between devices  39 us
    psum x1, waiting for transfers between devices, local(): lax.psum(grad_part.astype(jnp.bfloat16), 'dp').astype(jnp.float32)  34.9 us
    dot_general x25, matrix products, contract_last(): lax.dot_general(left, right, (((1,), (1,)), ((), ())), preferred_element_...  26.8 us
    all_gather x1, waiting for transfers between devices, local(): lax.all_gather(w_out, 'seq', axis=0, tiled=True)  24 us
    all_gather x1, waiting for transfers between devices, local(): lax.all_gather(w_key, 'seq', axis=0, tiled=True)  24 us
    all_gather x1, waiting for transfers between devices, local(): lax.all_gather(w_value, 'seq', axis=0, tiled=True)  23.2 us
    all_to_all x1, waiting for transfers between devices, _mix_targets(): return jnp.concatenate(jax.lax.all_to_all(local_out, which_axis, 0, 0), 2)  21.2 us
    dot_general x12, matrix products, local_apply(): near_out = jnp.dot(weights, value_one, preferred_element_type=jnp.float32)  18.7 us
  transfers between devices with their start and end apart: 11, of which 9 were waited for; matrix products, arithmetic and copies ran while one was open for 30% of the time, Pallas kernels for 0%

profile of v1, /device:TPU:0, one launch (start us, length us, event | category | flops | bytes accessed | tf_op | source)
XLA Modules:
  0.0 357.6 jit_solution(16604011389781454952)
XLA Ops:
  15.0 2.5 gather_fusion.1
  18.2 5.2 %all-to-all-start.1 = ((s32[8,2,20]{2,1,0:T(2,128)}), s32[8,2,20]{2,1,0:T(2,128)S(1)}, u32[]{:S(2)}, u32[]{:S(2)}) async-start(s32[8,2,20]{2,1,0:T(2,128)} %broadcast_select_fusion.2), calls=%async_computation.1 | async-start | bytes 16384 | tf_op jit(solution)/shard_map/all_to_all | solution.py:112
  23.4 13.1 %all-gather.5.cloned.1.call-done = bf16[768,768]{1,0:T(8,128)(2,1)} async-done(((bf16[96,768]{1,0:T(8,128)(2,1)}), bf16[768,768]{1,0:T(8,128)(2,1)}) %all-gather.5.cloned.1.call-update) | async-done | bytes 1179664 | tf_op jit(solution)/shard_map/all_gather | solution.py:47
  38.4 24.0 %all-gather.7.cloned.1.call-done = bf16[768,768]{1,0:T(8,128)(2,1)} async-done(((bf16[96,768]{1,0:T(8,128)(2,1)}), bf16[768,768]{1,0:T(8,128)(2,1)}) %all-gather.7.cloned.1.call-update) | async-done | bytes 1179664 | tf_op jit(solution)/shard_map/all_gather | solution.py:48
  65.0 23.2 %all-gather.9.cloned.1.call-done = bf16[768,768]{1,0:T(8,128)(2,1)} async-done(((bf16[96,768]{1,0:T(8,128)(2,1)}), bf16[768,768]{1,0:T(8,128)(2,1)}) %all-gather.9.cloned.1.call-update) | async-done | bytes 1179664 | tf_op jit(solution)/shard_map/all_gather | solution.py:49
  89.9 24.0 %all-gather.11.cloned.1.call-done = bf16[768,768]{1,0:T(8,128)(2,1)} async-done(((bf16[96,768]{1,0:T(8,128)(2,1)}), bf16[768,768]{1,0:T(8,128)(2,1)}) %all-gather.11.cloned.1.call-update) | async-done | bytes 1179664 | tf_op jit(solution)/shard_map/all_gather | solution.py:50
  117.3 4.4 %gather_fusion = bf16[320,4,768]{2,1,0:T(4,128)(2,1)} fusion(bf16[193,4,768]{2,1,0:T(4,128)(2,1)S(1)} %concatenate.16.clone, s32[1024]{0:T(1024)S(1)} %get-tuple-element.352), kind=kCustom, calls=%fused_computation | custom fusion | bytes 3933440 | tf_op jit(solution)/shard_map/jit(_take)/gather | solution.py:97
  121.7 2.4 select_convert_fusion
  131.9 14.4 %while.41 = (s32[]{:T(128)}, f32[12,192]{1,0:T(8,128)S(1)}, f32[12,192]{1,0:T(8,128)S(1)}, bf16[12,192,64]{2,1,0:T(8,128)(2,1)}, bf16[12,192,64]{2,1,0:T(8,128)(...) while((s32[]{:T(128)}, f32[12,192]{1,0:T(8,128)S(1)}, f32[12,192]{1,0:T(8,128)S(1)}, ...), condition=%wide.region_7.8_spmd.clone, body=%wide.region_4.7_spmd.clone.sunk | while | flops 4976258 | bytes 400221 | solution.py:82
  147.4 2.0 gather_fusion.2
  152.3 3.3 all-to-all-start.2
  156.5 4.0 %all-to-all-done.2 = f32[8,1,960]{2,1,0:T(1,128)S(1)} async-done(((f32[8,1,960]{2,1,0:T(1,128)}), f32[8,1,960]{2,1,0:T(1,128)S(1)}, u32[]{:S(2)}, u32[]{:S(2)}) %all-to-all-start.2) | async-done | bytes 30752 | tf_op jit(solution)/shard_map/all_to_all | solution.py:111
  160.5 3.8 %all-to-all-start = ((bf16[8,1,2,20,4,768]{5,4,3,2,1,0:T(4,128)(2,1)}), bf16[8,1,2,20,4,768]{5,4,3,2,1,0:T(4,128)(2,1)S(1)}, u32[]{:S(2)}, u32[]{:S(2)}) async-start(bf16[8,1,2,20,4,768]{5,4,3,2,1,0:T(4,128)(2,1)} %fusion.49), calls=%async_computation | async-start | bytes 3932160 | tf_op jit(solution)/shard_map/all_to_all | solution.py:16
  168.0 21.2 %all-to-all-done = bf16[8,1,2,20,4,768]{5,4,3,2,1,0:T(4,128)(2,1)S(1)} async-done(((bf16[8,1,2,20,4,768]{5,4,3,2,1,0:T(4,128)(2,1)}), bf16[8,1,2,20,4,768]{5,4,3,2,1,0:T(4,128)(2,1)S(1)}, u32[]{:S(2)}, u32[]{:S(2)}) %all-to-all-start) | async-done | bytes 1966112 | tf_op jit(solution)/shard_map/all_to_all | solution.py:16
  189.2 2.0 copy.131
  191.2 11.5 %while.42 = (s32[]{:T(128)}, bf16[2,160,768]{2,1,0:T(8,128)(2,1)}, bf16[2,160,768]{2,1,0:T(8,128)(2,1)}, f32[2,160,12]{1,2,0:T(8,128)S(1)}, bf16[2,160,4,768]{3,...) while((s32[]{:T(128)}, bf16[2,160,768]{2,1,0:T(8,128)(2,1)}, ...), condition=%wide.region_11.12_spmd.clone, body=%wide.region_8.11_spmd.clone.sunk | while | flops 121049760 | bytes 14496293 | solution.py:143
  203.7 3.3 all-to-all-start.3
  208.3 2.0 copy.154
  211.7 4.2 %all-to-all-start.4 = ((bf16[1,2,160,2,768]{4,3,1,0,2:T(2,128)(2,1)}), bf16[1,2,160,2,768]{4,3,1,0,2:T(2,128)(2,1)}, u32[]{:S(2)}, u32[]{:S(2)}) async-start(bf16[1,2,160,2,768]{4,3,1,0,2:T(2,128)(2,1)} %copy.154), calls=%async_computation.4 | async-start | bytes 1966080 | tf_op jit(solution)/shard_map/all_to_all | solution.py:147
  218.6 42.2 %while.43 = (s32[]{:T(128)}, f32[12,192,64]{1,2,0:T(8,128)}, bf16[12,192,64]{1,2,0:T(8,128)(2,1)S(1)}, bf16[12,192,64]{2,1,0:T(8,128)(2,1)}, bf16[12,192,64]{2,1...) while((s32[]{:T(128)}, f32[12,192,64]{1,2,0:T(8,128)}, ...), condition=%wide.region_13.14_spmd.clone, body=%wide.region_12.13_spmd.clone.sunk | while | flops 14376962 | bytes 546345 | solution.py:163
  264.8 3.1 gather_fusion.4
  270.9 2.4 copy.164
  274.8 36.4 %reduce-scatter.4.cloned.1.call-done = bf16[96,768]{1,0:T(8,128)(2,1)} async-done(((bf16[768,768]{1,0:T(8,128)(2,1)}), bf16[96,768]{1,0:T(8,128)(2,1)}) %reduce-scatter.4.cloned.1.call-update) | async-done | bytes 147472
  314.1 34.9 %all-reduce.5.cloned.1.call-done = bf16[96,768]{0,1:T(8,128)(2,1)} async-done(((bf16[96,768]{0,1:T(8,128)(2,1)}), bf16[96,768]{0,1:T(8,128)(2,1)}) %all-reduce.5.cloned.1.call-update) | async-done | bytes 147472 | tf_op jit(solution)/shard_map/psum | solution.py:183
  (242 shorter events, 120.4 us)
Async XLA Ops:
  7.2 29.4 %copy-start = (bf16[1,192,768]{2,1,0:T(8,128)(2,1)S(1)}, bf16[1,192,768]{2,1,0:T(8,128)(2,1)}, u32[]{:S(2)}) copy-start(bf16[1,192,768]{2,1,0:T(8,128)(2,1)} %param.14) | copy-start | bytes 884740
  7.2 29.4 %all-gather.5.cloned.1.call-start = ((), (), s32[]{:S(2)}) async-start(), calls=%async_computation.6 | async-start | bytes 1327104 | tf_op jit(solution)/shard_map/all_gather | solution.py:47
  7.9 54.5 %all-gather.7.cloned.1.call-start = ((), (), s32[]{:S(2)}) async-start(), calls=%async_computation.7 | async-start | bytes 1327104 | tf_op jit(solution)/shard_map/all_gather | solution.py:48
  8.7 79.6 %all-gather.9.cloned.1.call-start = ((), (), s32[]{:S(2)}) async-start(), calls=%async_computation.8 | async-start | bytes 1327104 | tf_op jit(solution)/shard_map/all_gather | solution.py:49
  9.4 104.5 %all-gather.11.cloned.1.call-start = ((), (), s32[]{:S(2)}) async-start(), calls=%async_computation.9 | async-start | bytes 1327104 | tf_op jit(solution)/shard_map/all_gather | solution.py:50
  18.2 134.1 %all-to-all-start.1 = ((s32[8,2,20]{2,1,0:T(2,128)}), s32[8,2,20]{2,1,0:T(2,128)S(1)}, u32[]{:S(2)}, u32[]{:S(2)}) async-start(s32[8,2,20]{2,1,0:T(2,128)} %broadcast_select_fusion.2), calls=%async_computation.1 | async-start | bytes 16384 | tf_op jit(solution)/shard_map/all_to_all | solution.py:112
  38.4 75.5 %copy-start.4 = (bf16[1,192,768]{2,1,0:T(8,128)(2,1)S(1)}, bf16[1,192,768]{2,1,0:T(8,128)(2,1)}, u32[]{:S(2)}) copy-start(bf16[1,192,768]{2,1,0:T(8,128)(2,1)} %param.15) | copy-start | bytes 884740
  146.3 0.8 copy-start.2
  152.3 8.1 %all-to-all-start.2 = ((f32[8,1,960]{2,1,0:T(1,128)}), f32[8,1,960]{2,1,0:T(1,128)S(1)}, u32[]{:S(2)}, u32[]{:S(2)}) async-start(f32[8,1,960]{2,1,0:T(1,128)} %reshape.248), calls=%async_computation.2 | async-start | bytes 65536 | tf_op jit(solution)/shard_map/all_to_all | solution.py:111
  156.5 7.8 %copy-start.5 = (s32[1,192,1]{1,2,0:T(1,128)S(1)}, s32[1,192,1]{1,2,0:T(1,128)}, u32[]{:S(2)}) copy-start(s32[1,192,1]{1,2,0:T(1,128)} %param.16) | copy-start | bytes 2308
  160.5 28.7 %all-to-all-start = ((bf16[8,1,2,20,4,768]{5,4,3,2,1,0:T(4,128)(2,1)}), bf16[8,1,2,20,4,768]{5,4,3,2,1,0:T(4,128)(2,1)S(1)}, u32[]{:S(2)}, u32[]{:S(2)}) async-start(bf16[8,1,2,20,4,768]{5,4,3,2,1,0:T(4,128)(2,1)} %fusion.49), calls=%async_computation | async-start | bytes 3932160 | tf_op jit(solution)/shard_map/all_to_all | solution.py:16
  203.7 8.0 %all-to-all-start.3 = ((f32[8,1,480]{2,1,0:T(1,128)}), f32[8,1,480]{2,1,0:T(1,128)S(1)}, u32[]{:S(2)}, u32[]{:S(2)}) async-start(f32[8,1,480]{2,1,0:T(1,128)} %reshape.250), calls=%async_computation.3 | async-start | bytes 32768 | tf_op jit(solution)/shard_map/all_to_all | solution.py:150
  210.3 8.3 %copy-start.3 = (bf16[12,192,64]{1,2,0:T(8,128)(2,1)S(1)}, bf16[12,192,64]{1,2,0:T(8,128)(2,1)}, u32[]{:S(2)}) copy-start(bf16[12,192,64]{1,2,0:T(8,128)(2,1)} %custom-call.17) | copy-start | bytes 884740
  211.7 49.6 %all-to-all-start.4 = ((bf16[1,2,160,2,768]{4,3,1,0,2:T(2,128)(2,1)}), bf16[1,2,160,2,768]{4,3,1,0,2:T(2,128)(2,1)}, u32[]{:S(2)}, u32[]{:S(2)}) async-start(bf16[1,2,160,2,768]{4,3,1,0,2:T(2,128)(2,1)} %copy.154), calls=%async_computation.4 | async-start | bytes 1966080 | tf_op jit(solution)/shard_map/all_to_all | solution.py:147
  215.9 95.3 %reduce-scatter.4.cloned.1.call-start = ((), (), s32[]{:S(2)}) async-start(), calls=%async_computation.11 | async-start | bytes 1327104
  273.3 39.7 %copy-start.1 = (bf16[768,768]{1,0:T(8,128)(2,1)S(1)}, bf16[768,768]{1,0:T(8,128)(2,1)}, u32[]{:S(2)}) copy-start(bf16[768,768]{1,0:T(8,128)(2,1)} %all-gather.11.cloned.1.call-done) | copy-start | bytes 3538948
  273.3 75.7 %all-reduce.5.cloned.1.call-start = ((), (), s32[]{:S(2)}) async-start(), calls=%async_computation.10 | async-start | bytes 393216 | tf_op jit(solution)/shard_map/psum | solution.py:183
Sparse Core Ops, SparseCore 0:
  9.9 26.6 all-gather.4
  38.4 23.9 all-gather.6
  64.3 23.9 all-gather.8
  90.0 23.9 all-gather.10
  273.4 37.7 reduce-scatter.3
  314.0 34.9 all-reduce.4
